TPU v7x, 128 devices: a whole 4x4x4 slice. The times are simulated.
128 devices in a mesh: wide: 16 (over z, x_lo, core), tall: 8 (over x_hi, y).
Axes of the slice: x: 4 (x_hi: 2, x_lo: 2; x = x_hi * 2 + x_lo), y: 4, z: 4, core: 2. Of those that a mesh axis runs over, the one named last changes fastest.
Arguments:
- initial: float32 [16384, 16384], P(('wide', 'tall')), as said below
- child_tiles: float32 [8192, 128, 128], P(('wide', 'tall')), may hold values from -0.75 to 0.75
- child_targets: int32 [8192, 2], P(('wide', 'tall')), may hold values from 0 to 127, as said below
Outputs:
- front: float32 [16384, 16384], P('tall', 'wide')
Inputs may be any that keep to these rules, and one draw needn't show every extreme that they name: initial is symmetric, and assembled with its lower triangle mirrored is positive definite. `child_targets`: tile t * 8 + k of a device (t < 8, k < 8) lands on a block whose rows lie in the 128 rows of initial held by device g * 8 + t, g being the sender's index along wide; such a block's grid owner is the device at tall index (block row * 1) mod 8 and wide index (block column * 128 // 512) mod 16; the 8 tiles of one device with the same t go to 8 different grid owners, so one device sends at most one tile to one owner; in every grid row some owner gets one tile from every device.
All inputs are finite; a program needn't handle non-finite values.
Results may differ from a plain program's by a relative error of at most 0.0003.
Values sent between devices are 32-bit elements; how exact they have to be, the bound alone decides.
A program may use at most 192 MiB of HBM per device.

v0:
```python
import jax
import jax.numpy as jnp
import numpy as np
from jax import lax
from jax.sharding import PartitionSpec as P

PANEL = 512
PANELS = 2
full_precision = lax.Precision.HIGHEST


def from_root(value, axis, source):
    kept = jnp.where(lax.axis_index(axis) == source, value, 0).astype(value.dtype)
    return lax.psum(kept, axis)


def add_blocks(base, tiles, block_index, tile_edge):
    base_rows, base_cols = base.shape
    row_count = base_rows // tile_edge
    col_count = base_cols // tile_edge
    slot_ids = jnp.arange(row_count * col_count, dtype=jnp.int32)
    selector = (slot_ids[:, None] == block_index[None, :]).astype(jnp.float32)
    summed = jnp.dot(selector, tiles, precision=full_precision, preferred_element_type=jnp.float32)
    summed = summed.reshape(row_count, col_count, tile_edge, tile_edge).transpose(0, 2, 1, 3)
    return base + summed.reshape(base_rows, base_cols)


def relayout(slab, wide_size, panel_width):
    slab_rows, front_order = slab.shape
    col_tiles = front_order // (panel_width * wide_size)
    pieces_out = slab.reshape(slab_rows, col_tiles, wide_size, panel_width)
    arrived = lax.all_to_all(pieces_out, "wide", split_axis=2, concat_axis=0, tiled=True)
    return arrived.reshape(wide_size * slab_rows, col_tiles * panel_width)


def share_strip(front_local, panel_at, panel_width):
    wide_size = lax.axis_size("wide")
    home_tile = panel_at // wide_size
    column_piece = lax.slice_in_dim(
        front_local, home_tile * panel_width, (home_tile + 1) * panel_width, axis=1
    )
    return from_root(column_piece, "wide", panel_at % wide_size)


def block_tables(wanted, tall_size):
    owners = wanted % tall_size
    slots_at = wanted // tall_size
    width_wanted = wanted.shape[1]
    same_owner = owners[:, :, None] == owners[:, None, :]
    earlier = np.tril(np.ones((width_wanted, width_wanted), dtype=np.int32), -1)[None, :, :] > 0
    ranks = np.sum(same_owner & earlier, axis=2)
    piece_depth = int(np.max(ranks)) + 1
    talls = np.arange(tall_size)
    places = np.arange(piece_depth)
    matches = (owners[:, None, None, :] == talls[None, :, None, None]) & (
        ranks[:, None, None, :] == places[None, None, :, None]
    )
    senders = np.sum(matches * slots_at[:, None, None, :], axis=3).astype(np.int32)
    receivers = (owners * piece_depth + ranks).astype(np.int32)
    return (senders, receivers)


def owned_piece(source, senders, group_at, tall_at, slab_rows):
    slot_count = source.shape[0] // slab_rows
    blocks = source.reshape(slot_count, slab_rows, source.shape[1])
    chosen = jnp.asarray(senders)[group_at, tall_at]
    return jnp.take(blocks, chosen, axis=0)


def order_rows(gathered, receivers, group_at):
    placed = jnp.take(gathered, jnp.asarray(receivers)[group_at], axis=0)
    return placed.reshape(placed.shape[0] * placed.shape[1], placed.shape[2])


def body(initial, child_tiles, child_targets):
    wide_size = lax.axis_size("wide")
    tall_size = lax.axis_size("tall")
    wide_at = lax.axis_index("wide")
    tall_at = lax.axis_index("tall")
    slab_rows, front_order = initial.shape
    tile_count, tile_edge, _ = child_tiles.shape
    per_row = tile_count // tall_size
    panel_width = PANEL
    col_tiles = front_order // (panel_width * wide_size)
    blocks_per_panel = panel_width // slab_rows
    flat_tiles = child_tiles.reshape(tile_count, tile_edge * tile_edge)
    front_local = relayout(initial, wide_size, panel_width)
    target_wide = child_targets[:, 1] * tile_edge // panel_width % wide_size
    target_tall = jnp.arange(tile_count, dtype=jnp.int32) // per_row
    target_slot = target_wide * tall_size + target_tall
    slot_ids = jnp.arange(wide_size * tall_size, dtype=jnp.int32)
    selector = slot_ids[:, None] == target_slot[None, :]
    buffer = jnp.dot(
        selector.astype(jnp.float32),
        flat_tiles,
        precision=full_precision,
        preferred_element_type=jnp.float32,
    )
    filled = jnp.any(selector, axis=1)
    placed = jnp.sum(selector.astype(jnp.int32)[:, :, None] * child_targets[None, :, :], axis=1)
    placed = jnp.where(filled[:, None], placed, -1)
    arrived, targets = (
        lax.all_to_all(buffer, ("wide", "tall"), split_axis=0, concat_axis=0, tiled=True),
        lax.all_to_all(placed, ("wide", "tall"), split_axis=0, concat_axis=0, tiled=True),
    )
    usable = targets[:, 0] >= 0
    row_global = targets[:, 0] * tile_edge
    row_group = row_global // slab_rows
    local_row = row_group // tall_size * slab_rows + row_global % slab_rows
    col_global = targets[:, 1] * tile_edge
    local_col = col_global // panel_width // wide_size * panel_width + col_global % panel_width
    grid_index = (
        local_row // tile_edge * (col_tiles * panel_width // tile_edge) + local_col // tile_edge
    )
    grid_index = jnp.where(usable, grid_index, -1)
    front_local = add_blocks(front_local, arrived, grid_index, tile_edge)
    local_index = jnp.arange(front_local.shape[0], dtype=jnp.int32)
    global_row = (
        local_index // slab_rows * tall_size + tall_at
    ) * slab_rows + local_index % slab_rows
    tile_steps = np.arange(col_tiles)
    inner_steps = np.arange(blocks_per_panel)
    wide_steps = np.arange(wide_size)
    solved_wanted = (
        (tile_steps[None, :, None] * wide_size + wide_steps[:, None, None]) * blocks_per_panel
        + inner_steps[None, None, :]
    ).reshape(wide_size, col_tiles * blocks_per_panel)
    solved_send, solved_receive = block_tables(solved_wanted, tall_size)
    identity = jnp.eye(panel_width, dtype=jnp.float32)
    column_strip = share_strip(front_local, 0, panel_width)
    for panel_at in range(PANELS):
        low_row = panel_at * panel_width
        high_row = low_row + panel_width
        diag_wanted = (np.arange(blocks_per_panel) + low_row // slab_rows)[None, :]
        diag_send, diag_receive = block_tables(diag_wanted, tall_size)
        diag_piece = owned_piece(column_strip, diag_send, 0, tall_at, slab_rows)
        diag_block = order_rows(
            lax.all_gather(diag_piece, "tall", axis=0, tiled=True), diag_receive, 0
        )
        factor = jnp.linalg.cholesky(jnp.tril(diag_block) + jnp.tril(diag_block, -1).T)
        inverse = lax.linalg.triangular_solve(factor, identity, left_side=True, lower=True)
        solved = jnp.dot(
            column_strip, inverse.T, precision=full_precision, preferred_element_type=jnp.float32
        )
        below_mask = (global_row >= high_row)[:, None]
        inside = ((global_row >= low_row) & (global_row < high_row))[:, None]
        lower_rows = jnp.where(below_mask, solved, 0.0)
        new_diag = jnp.tril(factor) + jnp.triu(diag_block, 1)
        diag_rows = jnp.take(new_diag, jnp.clip(global_row - low_row, 0, panel_width - 1), axis=0)
        new_strip = jnp.where(below_mask, solved, jnp.where(inside, diag_rows, column_strip))
        solved_piece = owned_piece(lower_rows, solved_send, wide_at, tall_at, slab_rows)
        column_rows = order_rows(
            lax.all_gather(solved_piece, "tall", axis=0, tiled=True), solved_receive, wide_at
        )
        root_wide = panel_at % wide_size
        home_tile = panel_at // wide_size
        has_next = panel_at + 1 < PANELS
        change = jnp.dot(
            lower_rows, column_rows.T, precision=full_precision, preferred_element_type=jnp.float32
        )
        front_local = front_local - change
        current = lax.slice_in_dim(
            front_local, home_tile * panel_width, (home_tile + 1) * panel_width, axis=1
        )
        front_local = front_local.at[
            :, home_tile * panel_width : (home_tile + 1) * panel_width
        ].set(jnp.where(wide_at == root_wide, new_strip, current))
        if has_next:
            column_strip = share_strip(front_local, panel_at + 1, panel_width)
    return front_local


def solution(mesh):
    return jax.shard_map(
        body,
        mesh=mesh,
        in_specs=(
            P(("wide", "tall"), None),
            P(("wide", "tall"), None, None),
            P(("wide", "tall"), None),
        ),
        out_specs=P("tall", "wide"),
        check_vma=False,
    )
```

profile of v0, /device:TPU:1, one launch (start us, length us, event | category | flops | bytes accessed | tf_op | source)
XLA Modules:
  0.0 1217.4 jit_solution(8326474147539438546)
XLA Ops:
  8.9 11.5 all-to-all-start.1
  20.4 9.9 copy.62
  54.5 9.8 copy.41
  64.4 76.3 %all-to-all-done = f32[128,2,16,512]{3,1,0,2:T(2,128)} async-done(((f32[128,2,16,512]{3,1,0,2:T(2,128)}), f32[128,2,16,512]{3,1,0,2:T(2,128)}, u32[]{:S(2)}, u32[]{:S(2)}) %all-to-all-start) | async-done | bytes 8388640 | tf_op jit(solution)/shard_map/all_to_all | solution.py:32
  158.3 90.6 %all-to-all-done.2 = f32[128,1,16384]{2,1,0:T(1,128)} async-done(((f32[128,1,16384]{2,1,0:T(1,128)}), f32[128,1,16384]{2,1,0:T(1,128)}, u32[]{:S(2)}, u32[]{:S(2)}) %all-to-all-start.2) | async-done | bytes 8388640 | tf_op jit(solution)/shard_map/all_to_all | solution.py:103
  248.9 18.0 %copy.61 = f32[128,1,16384]{0,2,1:T(8,128)} copy(f32[128,1,16384]{2,1,0:T(1,128)} %all-to-all-done.2) | data formatting | bytes 16777216 | tf_op jit(solution)/shard_map/dot_general | solution.py:23
  266.9 11.2 fusion.82
  278.1 12.3 %bitcast_add_fusion = f32[2048,1024]{1,0:T(8,128)} fusion(f32[2048,1024]{1,0:T(8,128)} %bitcast.181, f32[256,8,8,128]{3,2,1,0:T(8,128)} %bitcast.182), kind=kLoop, calls=%fused_computation.13 | loop fusion | flops 2097152 | bytes 25165824 | tf_op jit(solution)/shard_map/add | solution.py:25
  295.1 135.9 %all-reduce.4.cloned.1.call-done = f32[2048,512]{1,0:T(8,128)} async-done(((f32[2048,512]{1,0:T(8,128)}), f32[2048,512]{1,0:T(8,128)}) %all-reduce.4.cloned.1.call-update) | async-done | bytes 4194320 | tf_op jit(solution)/shard_map/psum | solution.py:14
  435.2 52.7 %all-gather.5.cloned.1.call-done = f32[8,128,512]{2,1,0:T(8,128)} async-done(((f32[1,128,512]{2,1,0:T(8,128)}), f32[8,128,512]{2,1,0:T(8,128)}) %all-gather.5.cloned.1.call-update) | async-done | bytes 2097168 | tf_op jit(solution)/shard_map/all_gather | solution.py:138
  496.7 11.7 cholesky.286
  520.9 11.9 cholesky.305
  532.8 9.8 custom-call.28
  544.2 11.7 cholesky.326
  555.9 9.8 custom-call.29
  567.2 11.9 cholesky.343
  586.3 11.6 while.7
  597.8 39.3 %custom-call.30 = f32[4,128,128]{1,2,0:T(8,128)S(1)} custom-call(f32[4,128,128]{2,1,0:T(8,128)S(1)} %get-tuple-element.61), custom_call_target="InvertDiagBlocksLowerTriangular" | custom-call | tf_op jit(solution)/shard_map/triangular_solve/custom-call.3 | solution.py:141
  666.1 59.2 %all-gather.7.cloned.1.call-done = f32[16,128,512]{2,1,0:T(8,128)} async-done(((f32[2,128,512]{2,1,0:T(8,128)}), f32[16,128,512]{2,1,0:T(8,128)}) %all-gather.7.cloned.1.call-update) | async-done | bytes 4194320 | tf_op jit(solution)/shard_map/all_gather | solution.py:153
  730.4 17.0 %convolution_subtract_fusion.1 = f32[2048,1024]{1,0:T(8,128)S(1)} fusion(f32[2048,1024]{1,0:T(8,128)} %bitcast_add_fusion, f32[2048,512]{1,0:T(8,128)S(1)} %copy-done.1, f32[1024,512]{1,0:T(8,128)S(1)} %bitcast.191), kind=kOutput, calls=%fused_computation.25 | convolution fusion | flops 12886999040 | bytes 23068672 | tf_op jit(solution)/shard_map/dot_general | solution.py:158
  753.6 133.2 %all-reduce.6.cloned.1.call-done = f32[2048,512]{1,0:T(8,128)} async-done(((f32[2048,512]{1,0:T(8,128)}), f32[2048,512]{1,0:T(8,128)}) %all-reduce.6.cloned.1.call-update) | async-done | bytes 4194320 | tf_op jit(solution)/shard_map/psum | solution.py:14
  888.8 54.8 %all-gather.9.cloned.1.call-done = f32[8,128,512]{2,1,0:T(8,128)} async-done(((f32[1,128,512]{2,1,0:T(8,128)}), f32[8,128,512]{2,1,0:T(8,128)}) %all-gather.9.cloned.1.call-update) | async-done | bytes 2097168 | tf_op jit(solution)/shard_map/all_gather | solution.py:138
  952.6 11.7 cholesky.358
  976.9 11.7 cholesky.377
  988.6 10.0 custom-call.32
  1000.2 11.7 cholesky.398
  1011.9 9.8 custom-call.33
  1023.2 12.1 cholesky.415
  1042.9 10.8 while.8
  1053.7 39.3 %custom-call.34 = f32[4,128,128]{1,2,0:T(8,128)S(1)} custom-call(f32[4,128,128]{2,1,0:T(8,128)S(1)} %get-tuple-element.62), custom_call_target="InvertDiagBlocksLowerTriangular" | custom-call | tf_op jit(solution)/shard_map/triangular_solve/custom-call.3 | solution.py:141
  1125.3 55.8 %all-gather.11.cloned.1.call-done = f32[16,128,512]{2,1,0:T(8,128)} async-done(((f32[2,128,512]{2,1,0:T(8,128)}), f32[16,128,512]{2,1,0:T(8,128)}) %all-gather.11.cloned.1.call-update) | async-done | bytes 4194320 | tf_op jit(solution)/shard_map/all_gather | solution.py:153
  1186.2 17.8 %convolution_subtract_fusion = f32[2048,1024]{1,0:T(8,128)} fusion(f32[2048,1024]{1,0:T(8,128)} %constant_dynamic-update-slice_fusion.6, f32[2048,512]{1,0:T(8,128)S(1)} %copy-done.2, f32[1024,512]{1,0:T(8,128)S(1)} %bitcast.190), kind=kOutput, calls=%fused_computation.24 | convolution fusion | flops 12886999040 | bytes 23068672 | tf_op jit(solution)/shard_map/dot_general | solution.py:158
  (186 shorter events, 219.7 us)
Async XLA Ops:
  8.9 30.9 %all-to-all-start.1 = ((s32[128,1,2]{2,1,0:T(1,128)}), s32[128,1,2]{2,1,0:T(1,128)S(1)}, u32[]{:S(2)}, u32[]{:S(2)}) async-start(s32[128,1,2]{2,1,0:T(1,128)} %copy.40), calls=%async_computation.1 | async-start | bytes 131072 | tf_op jit(solution)/shard_map/all_to_all | solution.py:104
  39.7 100.9 %all-to-all-start = ((f32[128,2,16,512]{3,1,0,2:T(2,128)}), f32[128,2,16,512]{3,1,0,2:T(2,128)}, u32[]{:S(2)}, u32[]{:S(2)}) async-start(f32[128,2,16,512]{3,1,0,2:T(2,128)} %copy.39), calls=%async_computation | async-start | bytes 16777216 | tf_op jit(solution)/shard_map/all_to_all | solution.py:32
  140.6 108.2 %all-to-all-start.2 = ((f32[128,1,16384]{2,1,0:T(1,128)}), f32[128,1,16384]{2,1,0:T(1,128)}, u32[]{:S(2)}, u32[]{:S(2)}) async-start(f32[128,1,16384]{2,1,0:T(1,128)} %copy.41), calls=%async_computation.2 | async-start | bytes 16777216 | tf_op jit(solution)/shard_map/all_to_all | solution.py:103
  149.0 281.9 %all-reduce.4.cloned.1.call-start = ((), (), s32[]{:S(2)}) async-start(), calls=%async_computation.3 | async-start | bytes 8388608 | tf_op jit(solution)/shard_map/psum | solution.py:14
  295.1 192.8 %all-gather.5.cloned.1.call-start = ((), (), s32[]{:S(2)}) async-start(), calls=%async_computation.4 | async-start | bytes 2359296 | tf_op jit(solution)/shard_map/all_gather | solution.py:138
  432.7 292.6 %all-gather.7.cloned.1.call-start = ((), (), s32[]{:S(2)}) async-start(), calls=%async_computation.5 | async-start | bytes 4718592 | tf_op jit(solution)/shard_map/all_gather | solution.py:153
  495.7 1.0 copy-start.13
  579.1 4.7 copy-start.11
  637.2 6.0 copy-start.3
  655.9 230.9 %all-reduce.6.cloned.1.call-start = ((), (), s32[]{:S(2)}) async-start(), calls=%async_computation.6 | async-start | bytes 8388608 | tf_op jit(solution)/shard_map/psum | solution.py:14
  728.2 2.2 copy-start.1
  730.4 17.0 %copy-start.4 = (f32[2048,512]{1,0:T(8,128)S(1)}, f32[2048,512]{1,0:T(8,128)}, u32[]{:S(2)}) copy-start(f32[2048,512]{1,0:T(8,128)} %all-reduce.4.cloned.1.call-done) | copy-start | bytes 12582916
  730.4 17.0 %copy-start.7 = (f32[2048,512]{1,0:T(8,128)S(1)}, f32[2048,512]{1,0:T(8,128)}, u32[]{:S(2)}) copy-start(f32[2048,512]{1,0:T(8,128)} %gather_fusion.3) | copy-start | bytes 12582916
  730.4 17.1 %copy-start.8 = (f32[2048,512]{1,0:T(8,128)S(1)}, f32[2048,512]{1,0:T(8,128)}, u32[]{:S(2)}) copy-start(f32[2048,512]{1,0:T(8,128)} %get-tuple-element.120) | copy-start | bytes 12582916
  747.4 6.1 copy-start
  753.5 135.2 %copy-start.15 = (s32[4]{0:T(128)S(1)}, s32[4]{0:T(128)}, u32[]{:S(2)}) copy-start(s32[4]{0:T(128)} %constant.489) | copy-start | bytes 52
  753.5 190.0 %all-gather.9.cloned.1.call-start = ((), (), s32[]{:S(2)}) async-start(), calls=%async_computation.7 | async-start | bytes 2359296 | tf_op jit(solution)/shard_map/all_gather | solution.py:138
  888.5 292.6 %all-gather.11.cloned.1.call-start = ((), (), s32[]{:S(2)}) async-start(), calls=%async_computation.8 | async-start | bytes 4718592 | tf_op jit(solution)/shard_map/all_gather | solution.py:153
  951.6 1.1 copy-start.14
  1035.3 5.1 copy-start.12
  1093.0 6.0 copy-start.5
  1184.0 2.2 copy-start.2
  1186.2 17.8 %copy-start.6 = (f32[2048,512]{1,0:T(8,128)S(1)}, f32[2048,512]{1,0:T(8,128)}, u32[]{:S(2)}) copy-start(f32[2048,512]{1,0:T(8,128)} %all-reduce.6.cloned.1.call-done) | copy-start | bytes 12582916
  1186.2 17.8 %copy-start.9 = (f32[2048,512]{1,0:T(8,128)S(1)}, f32[2048,512]{1,0:T(8,128)}, u32[]{:S(2)}) copy-start(f32[2048,512]{1,0:T(8,128)} %gather_fusion.7) | copy-start | bytes 12582916
  1186.2 17.8 %copy-start.10 = (f32[2048,512]{1,0:T(8,128)S(1)}, f32[2048,512]{1,0:T(8,128)}, u32[]{:S(2)}) copy-start(f32[2048,512]{1,0:T(8,128)} %get-tuple-element.124) | copy-start | bytes 12582916
Sparse Core Ops, SparseCore 0:
  295.2 135.7 all-reduce.3
  433.3 54.5 all-gather.4
  656.1 69.1 all-gather.6
  753.7 133.0 all-reduce.5
  889.0 54.5 all-gather.8
  1111.9 69.1 all-gather.10
where the time goes:
time: 1230 us; the launch traced here: 1220 us
  waiting for transfers between devices  658 us (53%)
  other arithmetic  284 us (23%)
  local copies, waits for them, and re-layouts  132 us (11%)
  matrix products  95.1 us (8%)
  starting transfers between devices  27.6 us (2%)
  between operations  19.3 us (2%)
    psum x2, waiting for transfers between devices, from_root(): return lax.psum(kept, axis)  269 us
    another operation x29, other arithmetic, body(): jnp.linalg.cholesky(jnp.tril(diag_block) + jnp.tril(diag_block, -1).T)  159 us
    all_gather x2, waiting for transfers between devices, body(): lax.all_gather(solved_piece, 'tall', axis=0, tiled=True)  115 us
    all_gather x2, waiting for transfers between devices, body(): lax.all_gather(diag_piece, 'tall', axis=0, tiled=True)  107 us
    all_to_all x1, waiting for transfers between devices, body(): lax.all_to_all(buffer, ('wide', 'tall'), split_axis=0, concat_axis=0, til...  90.6 us
    another operation x4, other arithmetic, body(): lax.linalg.triangular_solve(factor, identity, left_side=True, lower=True)  78.7 us
    all_to_all x1, waiting for transfers between devices, relayout(): lax.all_to_all(pieces_out, 'wide', split_axis=2, concat_axis=0, tiled=True)  76.3 us
    dot_general x2, matrix products, body(): jnp.dot(lower_rows, column_rows.T, precision=full_precision, preferred_el...  34.8 us
  transfers between devices with their start and end apart: 9, of which 8 were waited for; matrix products, arithmetic and copies ran while one was open for 6% of the time, Pallas kernels for 0%

commit v1 on v0

--- a/solution.py
+++ b/solution.py
@@ -9,9 +9,14 @@
 full_precision = lax.Precision.HIGHEST
 
 
+def record_divide(along_axis, row_data):
+    raw_out = lax.all_gather(row_data, axis_name=along_axis).sum(axis=0)
+    return raw_out
+
+
 def from_root(value, axis, source):
     kept = jnp.where(lax.axis_index(axis) == source, value, 0).astype(value.dtype)
-    return lax.psum(kept, axis)
+    return record_divide(axis, kept)
 
 
 def add_blocks(base, tiles, block_index, tile_edge):

time: 1230 us -> 1660 us (1.35)
  waiting for transfers between devices: 658 us -> 1050 us
  other arithmetic: 284 us -> 330 us
    all_gather x0 -> x2, waiting for transfers between devices: none -> 658 us  [record_divide(): raw_out = lax.all_gather(row_data, axis_name=along_axis).sum(axis=0)]
    psum x2 -> x0, waiting for transfers between devices: 269 us -> none  [from_root(): return lax.psum(kept, axis)]
    reduce_sum x0 -> x2, other arithmetic: none -> 46.2 us  [record_divide(): raw_out = lax.all_gather(row_data, axis_name=along_axis).sum(axis=0)]
  transfers between devices with their start and end apart: 9 -> 9, of which waited for: 8 -> 8; matrix products, arithmetic and copies ran while one was open for 6% -> 4% of each run, Pallas kernels for 0% -> 0%
where the time goes in v1:
time: 1660 us; the launch traced here: 1650 us
  waiting for transfers between devices  1050 us (63%)
  other arithmetic  330 us (20%)
  local copies, waits for them, and re-layouts  133 us (8%)
  matrix products  95.1 us (6%)
  starting transfers between devices  27.6 us (2%)
  between operations  19.5 us (1%)
    all_gather x2, waiting for transfers between devices, record_divide(): raw_out = lax.all_gather(row_data, axis_name=along_axis).sum(axis=0)  658 us
    another operation x29, other arithmetic, body(): jnp.linalg.cholesky(jnp.tril(diag_block) + jnp.tril(diag_block, -1).T)  159 us
    all_gather x2, waiting for transfers between devices, body(): lax.all_gather(solved_piece, 'tall', axis=0, tiled=True)  114 us
    all_gather x2, waiting for transfers between devices, body(): lax.all_gather(diag_piece, 'tall', axis=0, tiled=True)  106 us
    all_to_all x1, waiting for transfers between devices, body(): lax.all_to_all(buffer, ('wide', 'tall'), split_axis=0, concat_axis=0, til...  90.6 us
    another operation x4, other arithmetic, body(): lax.linalg.triangular_solve(factor, identity, left_side=True, lower=True)  78.7 us
    all_to_all x1, waiting for transfers between devices, relayout(): lax.all_to_all(pieces_out, 'wide', split_axis=2, concat_axis=0, tiled=True)  76.3 us
    reduce_sum x2, other arithmetic, record_divide(): raw_out = lax.all_gather(row_data, axis_name=along_axis).sum(axis=0)  46.2 us
  transfers between devices with their start and end apart: 9, of which 8 were waited for; matrix products, arithmetic and copies ran while one was open for 4% of the time, Pallas kernels for 0%

profile of v1, /device:TPU:1, one launch (start us, length us, event | category | flops | bytes accessed | tf_op | source)
XLA Modules:
  0.0 1650.7 jit_solution(2472410711079009400)
XLA Ops:
  8.9 11.5 all-to-all-start.1
  20.4 9.9 copy.64
  64.4 76.3 %all-to-all-done = f32[128,2,16,512]{3,1,0,2:T(2,128)} async-done(((f32[128,2,16,512]{3,1,0,2:T(2,128)}), f32[128,2,16,512]{3,1,0,2:T(2,128)}, u32[]{:S(2)}, u32[]{:S(2)}) %all-to-all-start) | async-done | bytes 8388640 | tf_op jit(solution)/shard_map/all_to_all | solution.py:37
  158.3 90.6 %all-to-all-done.2 = f32[128,1,16384]{2,1,0:T(1,128)} async-done(((f32[128,1,16384]{2,1,0:T(1,128)}), f32[128,1,16384]{2,1,0:T(1,128)}, u32[]{:S(2)}, u32[]{:S(2)}) %all-to-all-start.2) | async-done | bytes 8388640 | tf_op jit(solution)/shard_map/all_to_all | solution.py:108
  248.9 18.0 %copy.63 = f32[128,1,16384]{0,2,1:T(8,128)} copy(f32[128,1,16384]{2,1,0:T(1,128)} %all-to-all-done.2) | data formatting | bytes 16777216 | tf_op jit(solution)/shard_map/dot_general | solution.py:28
  266.9 11.2 fusion.82
  278.1 12.3 bitcast_add_fusion
  295.1 330.1 %all-gather.17.cloned.1.call-done = f32[32768,512]{1,0:T(8,128)} async-done(((f32[2048,512]{1,0:T(8,128)}), f32[32768,512]{1,0:T(8,128)}) %all-gather.17.cloned.1.call-update) | async-done | bytes 67108880 | tf_op jit(solution)/shard_map/all_gather | solution.py:13
  625.2 23.1 %reduce_sum.31 = f32[2048,512]{1,0:T(8,128)} reduce(f32[16,2048,512]{2,1,0:T(8,128)} %bitcast.12, f32[]{:T(128)} %constant.398.clone.1), dimensions={0}, to_apply=%region_2.3 | reduce | flops 15728640 | bytes 71303168 | tf_op jit(solution)/shard_map/reduce_sum | solution.py:13
  651.8 52.3 %all-gather.9.cloned.1.call-done = f32[8,128,512]{2,1,0:T(8,128)} async-done(((f32[1,128,512]{2,1,0:T(8,128)}), f32[8,128,512]{2,1,0:T(8,128)}) %all-gather.9.cloned.1.call-update) | async-done | bytes 2097168 | tf_op jit(solution)/shard_map/all_gather | solution.py:143
  713.0 11.7 cholesky.286
  737.2 11.8 cholesky.305
  749.1 9.8 custom-call.28
  760.5 11.7 cholesky.326
  783.5 11.9 cholesky.343
  802.6 11.3 while.7
  813.9 39.3 %custom-call.30 = f32[4,128,128]{1,2,0:T(8,128)S(1)} custom-call(f32[4,128,128]{2,1,0:T(8,128)S(1)} %get-tuple-element.61), custom_call_target="InvertDiagBlocksLowerTriangular" | custom-call | tf_op jit(solution)/shard_map/triangular_solve/custom-call.3 | solution.py:146
  882.7 58.5 %all-gather.11.cloned.1.call-done = f32[16,128,512]{2,1,0:T(8,128)} async-done(((f32[2,128,512]{2,1,0:T(8,128)}), f32[16,128,512]{2,1,0:T(8,128)}) %all-gather.11.cloned.1.call-update) | async-done | bytes 4194320 | tf_op jit(solution)/shard_map/all_gather | solution.py:158
  946.3 17.0 %convolution_subtract_fusion.1 = f32[2048,1024]{1,0:T(8,128)S(1)} fusion(f32[2048,1024]{1,0:T(8,128)} %bitcast_add_fusion, f32[2048,512]{1,0:T(8,128)S(1)} %copy-done.5, f32[1024,512]{1,0:T(8,128)S(1)} %bitcast.193), kind=kOutput, calls=%fused_computation.25 | convolution fusion | flops 12886999040 | bytes 23068672 | tf_op jit(solution)/shard_map/dot_general | solution.py:163
  969.5 327.5 %all-gather.19.cloned.1.call-done = f32[32768,512]{1,0:T(8,128)} async-done(((f32[2048,512]{1,0:T(8,128)}), f32[32768,512]{1,0:T(8,128)}) %all-gather.19.cloned.1.call-update) | async-done | bytes 67108880 | tf_op jit(solution)/shard_map/all_gather | solution.py:13
  1297.0 23.1 %reduce_sum.32 = f32[2048,512]{1,0:T(8,128)} reduce(f32[16,2048,512]{2,1,0:T(8,128)} %bitcast.31, f32[]{:T(128)} %constant.398.clone.1), dimensions={0}, to_apply=%region_12.20 | reduce | flops 15728640 | bytes 71303168 | tf_op jit(solution)/shard_map/reduce_sum | solution.py:13
  1322.1 53.9 %all-gather.13.cloned.1.call-done = f32[8,128,512]{2,1,0:T(8,128)} async-done(((f32[1,128,512]{2,1,0:T(8,128)}), f32[8,128,512]{2,1,0:T(8,128)}) %all-gather.13.cloned.1.call-update) | async-done | bytes 2097168 | tf_op jit(solution)/shard_map/all_gather | solution.py:143
  1384.8 11.7 cholesky.358
  1409.0 11.7 cholesky.377
  1420.8 10.0 custom-call.32
  1432.4 11.7 cholesky.398
  1444.1 9.8 custom-call.33
  1455.4 12.1 cholesky.415
  1475.3 11.7 while.8
  1487.1 39.3 %custom-call.34 = f32[4,128,128]{1,2,0:T(8,128)S(1)} custom-call(f32[4,128,128]{2,1,0:T(8,128)S(1)} %get-tuple-element.62), custom_call_target="InvertDiagBlocksLowerTriangular" | custom-call | tf_op jit(solution)/shard_map/triangular_solve/custom-call.3 | solution.py:146
  1558.8 55.7 %all-gather.15.cloned.1.call-done = f32[16,128,512]{2,1,0:T(8,128)} async-done(((f32[2,128,512]{2,1,0:T(8,128)}), f32[16,128,512]{2,1,0:T(8,128)}) %all-gather.15.cloned.1.call-update) | async-done | bytes 4194320 | tf_op jit(solution)/shard_map/all_gather | solution.py:158
  1619.5 17.8 %convolution_subtract_fusion = f32[2048,1024]{1,0:T(8,128)} fusion(f32[2048,1024]{1,0:T(8,128)} %constant_dynamic-update-slice_fusion.6, f32[2048,512]{1,0:T(8,128)S(1)} %copy-done.6, f32[1024,512]{1,0:T(8,128)S(1)} %bitcast.192), kind=kOutput, calls=%fused_computation.24 | convolution fusion | flops 12886999040 | bytes 23068672 | tf_op jit(solution)/shard_map/dot_general | solution.py:163
  (189 shorter events, 239.8 us)
Async XLA Ops:
  8.9 30.9 %all-to-all-start.1 = ((s32[128,1,2]{2,1,0:T(1,128)}), s32[128,1,2]{2,1,0:T(1,128)S(1)}, u32[]{:S(2)}, u32[]{:S(2)}) async-start(s32[128,1,2]{2,1,0:T(1,128)} %copy.40), calls=%async_computation.1 | async-start | bytes 131072 | tf_op jit(solution)/shard_map/all_to_all | solution.py:109
  39.7 100.9 %all-to-all-start = ((f32[128,2,16,512]{3,1,0,2:T(2,128)}), f32[128,2,16,512]{3,1,0,2:T(2,128)}, u32[]{:S(2)}, u32[]{:S(2)}) async-start(f32[128,2,16,512]{3,1,0,2:T(2,128)} %copy.39), calls=%async_computation | async-start | bytes 16777216 | tf_op jit(solution)/shard_map/all_to_all | solution.py:37
  140.6 108.2 %all-to-all-start.2 = ((f32[128,1,16384]{2,1,0:T(1,128)}), f32[128,1,16384]{2,1,0:T(1,128)}, u32[]{:S(2)}, u32[]{:S(2)}) async-start(f32[128,1,16384]{2,1,0:T(1,128)} %copy.41), calls=%async_computation.2 | async-start | bytes 16777216 | tf_op jit(solution)/shard_map/all_to_all | solution.py:108
  149.0 476.1 %all-gather.17.cloned.1.call-start = ((), (), s32[]{:S(2)}) async-start(), calls=%async_computation.7 | async-start | bytes 71303168 | tf_op jit(solution)/shard_map/all_gather | solution.py:13
  295.1 409.1 %all-gather.9.cloned.1.call-start = ((), (), s32[]{:S(2)}) async-start(), calls=%async_computation.3 | async-start | bytes 2359296 | tf_op jit(solution)/shard_map/all_gather | solution.py:143
  650.0 291.3 %all-gather.11.cloned.1.call-start = ((), (), s32[]{:S(2)}) async-start(), calls=%async_computation.4 | async-start | bytes 4718592 | tf_op jit(solution)/shard_map/all_gather | solution.py:158
  712.0 1.0 copy-start.13
  795.4 4.7 copy-start.11
  853.2 6.1 copy-start.1
  871.9 425.1 %all-gather.19.cloned.1.call-start = ((), (), s32[]{:S(2)}) async-start(), calls=%async_computation.8 | async-start | bytes 71303168 | tf_op jit(solution)/shard_map/all_gather | solution.py:13
  944.2 2.2 copy-start.5
  946.3 17.0 %copy-start.2 = (f32[2048,512]{1,0:T(8,128)S(1)}, f32[2048,512]{1,0:T(8,128)}, u32[]{:S(2)}) copy-start(f32[2048,512]{1,0:T(8,128)} %reduce_sum.31) | copy-start | bytes 12582916
  946.3 17.0 %copy-start.7 = (f32[2048,512]{1,0:T(8,128)S(1)}, f32[2048,512]{1,0:T(8,128)}, u32[]{:S(2)}) copy-start(f32[2048,512]{1,0:T(8,128)} %gather_fusion.3) | copy-start | bytes 12582916
  946.3 17.1 %copy-start.8 = (f32[2048,512]{1,0:T(8,128)S(1)}, f32[2048,512]{1,0:T(8,128)}, u32[]{:S(2)}) copy-start(f32[2048,512]{1,0:T(8,128)} %get-tuple-element.120) | copy-start | bytes 12582916
  963.4 6.0 copy-start
  969.4 406.6 %all-gather.13.cloned.1.call-start = ((), (), s32[]{:S(2)}) async-start(), calls=%async_computation.5 | async-start | bytes 2359296 | tf_op jit(solution)/shard_map/all_gather | solution.py:143
  1297.0 25.0 %copy-start.15 = (s32[4]{0:T(128)S(1)}, s32[4]{0:T(128)}, u32[]{:S(2)}) copy-start(s32[4]{0:T(128)} %constant.489) | copy-start | bytes 52
  1321.8 292.7 %all-gather.15.cloned.1.call-start = ((), (), s32[]{:S(2)}) async-start(), calls=%async_computation.6 | async-start | bytes 4718592 | tf_op jit(solution)/shard_map/all_gather | solution.py:158
  1383.8 1.0 copy-start.14
  1467.5 5.4 copy-start.12
  1526.4 6.1 copy-start.3
  1617.3 2.2 copy-start.6
  1619.5 17.8 %copy-start.4 = (f32[2048,512]{1,0:T(8,128)S(1)}, f32[2048,512]{1,0:T(8,128)}, u32[]{:S(2)}) copy-start(f32[2048,512]{1,0:T(8,128)} %reduce_sum.32) | copy-start | bytes 12582916
  1619.5 17.8 %copy-start.9 = (f32[2048,512]{1,0:T(8,128)S(1)}, f32[2048,512]{1,0:T(8,128)}, u32[]{:S(2)}) copy-start(f32[2048,512]{1,0:T(8,128)} %gather_fusion.7) | copy-start | bytes 12582916
  1619.5 17.8 %copy-start.10 = (f32[2048,512]{1,0:T(8,128)S(1)}, f32[2048,512]{1,0:T(8,128)}, u32[]{:S(2)}) copy-start(f32[2048,512]{1,0:T(8,128)} %get-tuple-element.124) | copy-start | bytes 12582916
Sparse Core Ops, SparseCore 0:
  295.2 329.9 all-gather.16
  650.1 54.0 all-gather.8
  872.0 69.1 all-gather.10
  969.5 327.4 all-gather.18
  1321.9 54.0 all-gather.12
  1545.2 69.1 all-gather.14
